TPU v7x, 512 devices: a whole 4x4x16 slice. The times are simulated.
512 devices in a mesh: region: 64 (over z, x), split: 8 (over y, core).
Axes of the slice: x: 4, y: 4, z: 16, core: 2. Of those that a mesh axis runs over, the one named last changes fastest.
Arguments:
- vectors: float32 [294912, 256], P(('region', 'split'))
- hessian: bfloat16 [1536, 12, 192, 192], P(('region', 'split')), may hold values from -0.125 to 0.125
- block_cols: int32 [1536, 12], P(('region', 'split')), may hold values from 0 to 35, as said below
- live_blocks: int32 [1536], P(('region', 'split')), may hold values from 6 to 12, as said below
- halo_lists: int32 [64, 2, 6], P('region'), may hold values from 0 to 23, as said below
- bounds: float32 [2], replicated, as said below
Outputs:
- basis: float32 [294912, 256], P(('region', 'split'))
- projected: float32 [256, 256], replicated
Inputs may be any that keep to these rules, and one draw needn't show every extreme that they name: `block_cols`: in each row the entries are distinct and entry 0 is the row's own block within its region; values below 24 name blocks of the row's region, 24 + j the j-th block received from the lower region, 30 + j the j-th from the upper region. `live_blocks`: the first block row of every region has all 12 blocks intact. `halo_lists`: each list holds distinct block indices within the region. bounds[0] < 0 < bounds[1].
All inputs are finite; a program needn't handle non-finite values.
Results may differ from a plain program's by a relative error of at most 0.0005.
The roundings to bfloat16 on the way count: a program that leaves them out, or rounds other values in their place, can miss the bound.
Values may be sent and summed in bfloat16 or wider, within the bound.
A program may use at most 64 MiB of HBM per device.

v0:
```python
import jax
import jax.numpy as jnp
from jax import lax
from jax.sharding import PartitionSpec as P


def shifted(value, axis, steps):
    count = lax.axis_size(axis)
    pairs = [(source, (source + steps) % count) for source in range(count)]
    return lax.ppermute(value, axis, pairs)


def apply_blocks(operand, hessian, block_cols, live_blocks, halo_lists):
    row_blocks = hessian.shape[0]
    block_size = hessian.shape[2]
    mode_count = operand.shape[1]
    shard_blocks = operand.reshape(row_blocks, block_size, mode_count)
    region = lax.all_gather(shard_blocks, "split", axis=0, tiled=True)
    send_lower = region[halo_lists[0, 0]]
    send_upper = region[halo_lists[0, 1]]
    from_lower = shifted(send_upper, "region", 1)
    from_upper = shifted(send_lower, "region", -1)
    candidates = jnp.concatenate([region, from_lower, from_upper], 0)
    picked = candidates[block_cols]
    used_mask = lax.broadcasted_iota(jnp.int32, block_cols.shape, 1) < live_blocks[:, None]
    picked = jnp.where(used_mask[:, :, None, None], picked, jnp.zeros((), jnp.bfloat16))
    product = jnp.einsum("rkij,rkjm->rim", hessian, picked, preferred_element_type=jnp.float32)
    return product.reshape(row_blocks * block_size, mode_count)


def local(vectors, hessian, block_cols, live_blocks, halo_lists, bounds):
    centre = 0.5 * (bounds[0] + bounds[1])
    half_width = 0.5 * (bounds[1] - bounds[0])
    first = apply_blocks(vectors.astype(jnp.bfloat16), hessian, block_cols, live_blocks, halo_lists)
    filtered_one = (first - centre * vectors) / half_width
    second = apply_blocks(
        filtered_one.astype(jnp.bfloat16), hessian, block_cols, live_blocks, halo_lists
    )
    filtered_two = 2.0 * (second - centre * filtered_one) / half_width - vectors
    image = apply_blocks(
        filtered_two.astype(jnp.bfloat16), hessian, block_cols, live_blocks, halo_lists
    )
    total_rows = vectors.shape[0] * lax.axis_size("region") * lax.axis_size("split")
    contract = (((0,), (0,)), ((), ()))
    gram_part = lax.dot_general(
        filtered_two, filtered_two, contract, precision=lax.Precision.HIGHEST
    )
    cross_part = lax.dot_general(filtered_two, image, contract, precision=lax.Precision.HIGHEST)
    gram, cross = lax.psum((gram_part, cross_part), ("region", "split"))
    gram = gram / total_rows
    cross = cross / total_rows
    lower = jnp.linalg.cholesky(gram)
    basis = jax.scipy.linalg.solve_triangular(lower, filtered_two.T, lower=True).T
    partial_left = jax.scipy.linalg.solve_triangular(lower, cross, lower=True)
    projected = jax.scipy.linalg.solve_triangular(lower, partial_left.T, lower=True).T
    return (basis, projected)


def solution(mesh):
    placed = (
        P(("region", "split"), None),
        P(("region", "split"), None, None, None),
        P(("region", "split"), None),
        P(("region", "split")),
        P("region", None, None),
        P(),
    )
    return jax.shard_map(
        local,
        mesh=mesh,
        in_specs=placed,
        out_specs=(P(("region", "split"), None), P()),
        check_vma=False,
    )
```

profile of v0, /device:TPU:1, one launch (start us, length us, event | category | flops | bytes accessed | tf_op | source)
XLA Modules:
  0.0 814.2 jit_solution(8782221556383976657)
XLA Ops:
  7.2 2.0 convert_element_type.9
  9.3 0.8 fusion.33
  10.1 39.6 %all-gather.4.cloned.1.call-done = bf16[24,192,256]{2,1,0:T(8,128)(2,1)} async-done(((bf16[3,192,256]{2,1,0:T(8,128)(2,1)}), bf16[24,192,256]{2,1,0:T(8,128)(2,1)}) %all-gather.4.cloned.1.call-update) | async-done | bytes 2359312 | tf_op jit(solution)/shard_map/all_gather | solution.py:18
  49.7 3.1 gather_fusion
  52.8 3.1 collective-permute-start
  55.9 3.1 gather_fusion.1
  59.0 6.6 collective-permute-start.1
  69.7 4.6 collective-permute-done
  74.3 4.0 collective-permute-done.1
  78.3 3.4 pad_maximum_fusion
  81.7 4.8 gather_fusion.2
  86.6 3.0 fusion.4
  89.6 0.9 fusion.19
  90.6 34.4 %all-gather.6.cloned.1.call-done = bf16[24,192,256]{2,1,0:T(8,128)(2,1)} async-done(((bf16[3,192,256]{2,1,0:T(8,128)(2,1)}), bf16[24,192,256]{2,1,0:T(8,128)(2,1)}) %all-gather.6.cloned.1.call-update) | async-done | bytes 2359312 | tf_op jit(solution)/shard_map/all_gather | solution.py:18
  125.0 3.1 gather_fusion.3
  128.1 3.1 collective-permute-start.2
  131.2 3.1 gather_fusion.4
  134.3 6.6 collective-permute-start.3
  141.0 8.7 %collective-permute-done.2 = bf16[6,192,256]{2,1,0:T(8,128)(2,1)} collective-permute-done((bf16[6,192,256]{2,1,0:T(8,128)(2,1)}, bf16[6,192,256]{2,1,0:T(8,128)(2,1)}, u32[]{:S(2)}, u32[]{:S(2)}) %collective-permute-start.2) | collective-permute-done | bytes 589856 | tf_op jit(solution)/shard_map/ppermute | solution.py:10
  149.7 4.0 collective-permute-done.3
  153.7 3.3 pad_maximum_fusion.1
  157.0 4.8 gather_fusion.5
  161.9 3.1 fusion.2
  164.9 1.1 fusion.38
  166.1 34.3 %all-gather.8.cloned.1.call-done = bf16[24,192,256]{2,1,0:T(8,128)(2,1)} async-done(((bf16[3,192,256]{2,1,0:T(8,128)(2,1)}), bf16[24,192,256]{2,1,0:T(8,128)(2,1)}) %all-gather.8.cloned.1.call-update) | async-done | bytes 2359312 | tf_op jit(solution)/shard_map/all_gather | solution.py:18
  200.5 3.1 gather_fusion.6
  203.6 3.1 collective-permute-start.4
  206.7 3.1 gather_fusion.7
  209.8 6.6 collective-permute-start.5
  216.4 3.2 fusion.42
  219.6 5.5 collective-permute-done.4
  225.1 4.0 collective-permute-done.5
  229.1 3.3 pad_maximum_fusion.2
  232.5 4.8 gather_fusion.8
  237.3 3.0 fusion
  240.3 1.9 fusion.43
  242.3 466.4 %all-reduce.4.cloned.1.call-done = (f32[256,256]{0,1:T(8,128)}, f32[256,256]{0,1:T(8,128)}) async-done(((f32[256,256]{0,1:T(8,128)}, f32[256,256]{0,1:T(8,128)}), (f32[256,256]{0,1:T(8,128)}, f32[256,256]{0,1:T(8,128)})) %all-reduce.4.cloned.1.call-update) | async-done | bytes 524304 | tf_op jit(solution)/shard_map/psum | solution.py:49
  708.8 1.9 broadcast_multiply_fusion
  710.6 1.8 copy.13
  712.4 1.1 fusion.18
  714.8 13.2 %cholesky.50 = f32[128,128]{1,0:T(8,128)} custom-call(f32[128,128]{1,0:T(8,128)} %cholesky.118), custom_call_target="Cholesky" | custom-call | tf_op jit(solution)/shard_map/jit(cholesky)/cholesky | solution.py:52
  728.0 1.5 select_reduce_fusion.1
  729.5 1.6 cholesky.113
  731.0 11.3 %custom-call.18 = f32[1,128,128]{1,2,0:T(8,128)} custom-call(f32[1,128,128]{2,1,0:T(8,128)} %get-tuple-element.48), custom_call_target="InvertDiagBlocksLowerTriangular" | custom-call | tf_op jit(solution)/shard_map/jit(cholesky)/cholesky | solution.py:52
  742.3 1.7 constant_dynamic-update-slice_fusion.1
  744.0 1.7 convolution_subtract_fusion.3
  745.7 13.4 %cholesky.105 = f32[128,128]{1,0:T(8,128)} custom-call(f32[128,128]{1,0:T(8,128)} %convolution_subtract_fusion.3), custom_call_target="Cholesky" | custom-call | tf_op jit(solution)/shard_map/jit(cholesky)/cholesky | solution.py:52
  759.1 1.5 select_reduce_fusion
  763.2 1.7 select_select_fusion
  765.0 6.9 while.5
  765.6 2.9 bitcast_dynamic-update-slice_fusion.2
  769.0 2.8 bitcast_dynamic-update-slice_fusion.2
  771.8 21.1 %custom-call.19 = f32[2,128,128]{1,2,0:T(8,128)} custom-call(f32[2,128,128]{2,1,0:T(8,128)} %get-tuple-element.18), custom_call_target="InvertDiagBlocksLowerTriangular" | custom-call | tf_op jit(solution)/shard_map/jit(_solve_triangular)/triangular_solve | solution.py:53
  792.9 1.3 fusion.22
  794.2 1.3 convolution_subtract_fusion.2
  795.5 1.1 fusion.28
  796.7 1.2 fusion.20
  797.9 1.2 convolution_subtract_fusion.1
  799.1 1.2 fusion.27
  801.0 1.8 copy.15
  802.8 1.4 fusion.16
  804.2 1.4 convolution_subtract_fusion
  805.6 1.2 fusion.29
  806.8 0.9 maximum_bitcast_fusion
  (45 shorter events, 6.4 us)
Async XLA Ops:
  7.2 79.4 %copy-start = (bf16[3,12,192,192]{3,2,1,0:T(8,128)(2,1)S(1)}, bf16[3,12,192,192]{3,2,1,0:T(8,128)(2,1)}, u32[]{:S(2)}) copy-start(bf16[3,12,192,192]{3,2,1,0:T(8,128)(2,1)} %param.9) | copy-start | bytes 7962628
  7.2 58.4 %copy-start.8 = (f32[2]{0:T(128)S(1)}, f32[2]{0:T(128)}, u32[]{:S(2)}) copy-start(f32[2]{0:T(128)} %param.13) | copy-start | bytes 28
  7.2 61.7 %copy-start.7 = (s32[3,12]{1,0:T(4,128)S(1)}, s32[3,12]{1,0:T(4,128)}, u32[]{:S(2)}) copy-start(s32[3,12]{1,0:T(4,128)} %param.10) | copy-start | bytes 436
  7.2 42.5 %all-gather.4.cloned.1.call-start = ((), (), s32[]{:S(2)}) async-start(), calls=%async_computation | async-start | bytes 2654208 | tf_op jit(solution)/shard_map/all_gather | solution.py:18
  9.2 115.8 %all-gather.6.cloned.1.call-start = ((), (), s32[]{:S(2)}) async-start(), calls=%async_computation.1 | async-start | bytes 2654208 | tf_op jit(solution)/shard_map/all_gather | solution.py:18
  52.8 21.5 %collective-permute-start = (bf16[6,192,256]{2,1,0:T(8,128)(2,1)}, bf16[6,192,256]{2,1,0:T(8,128)(2,1)}, u32[]{:S(2)}, u32[]{:S(2)}) collective-permute-start(bf16[6,192,256]{2,1,0:T(8,128)(2,1)} %gather_fusion), channel_id=1, source_target_pairs={{0,8},{8,16},{16,24},{24,32},{32,40},{40,48},{48,56},{56,64},{64,7... | collective-permute-start | bytes 1769480 | tf_op jit(solution)/shard_map/ppermute | solution.py:10
  59.0 19.3 %collective-permute-start.1 = (bf16[6,192,256]{2,1,0:T(8,128)(2,1)}, bf16[6,192,256]{2,1,0:T(8,128)(2,1)}, u32[]{:S(2)}, u32[]{:S(2)}) collective-permute-start(bf16[6,192,256]{2,1,0:T(8,128)(2,1)} %gather_fusion.1), channel_id=1, source_target_pairs={{0,504},{8,0},{16,8},{24,16},{32,24},{40,32},{48,40},{56,48},{64,5... | collective-permute-start | bytes 1769480 | tf_op jit(solution)/shard_map/ppermute | solution.py:10
  86.6 3.1 copy-start.2
  89.6 0.9 copy-start.4
  90.6 109.9 %all-gather.8.cloned.1.call-start = ((), (), s32[]{:S(2)}) async-start(), calls=%async_computation.2 | async-start | bytes 2654208 | tf_op jit(solution)/shard_map/all_gather | solution.py:18
  128.1 21.5 %collective-permute-start.2 = (bf16[6,192,256]{2,1,0:T(8,128)(2,1)}, bf16[6,192,256]{2,1,0:T(8,128)(2,1)}, u32[]{:S(2)}, u32[]{:S(2)}) collective-permute-start(bf16[6,192,256]{2,1,0:T(8,128)(2,1)} %gather_fusion.3), channel_id=1, source_target_pairs={{0,8},{8,16},{16,24},{24,32},{32,40},{40,48},{48,56},{56,64},{64,7... | collective-permute-start | bytes 1769480 | tf_op jit(solution)/shard_map/ppermute | solution.py:10
  134.3 19.3 %collective-permute-start.3 = (bf16[6,192,256]{2,1,0:T(8,128)(2,1)}, bf16[6,192,256]{2,1,0:T(8,128)(2,1)S(1)}, u32[]{:S(2)}, u32[]{:S(2)}) collective-permute-start(bf16[6,192,256]{2,1,0:T(8,128)(2,1)} %gather_fusion.4), channel_id=1, source_target_pairs={{0,504},{8,0},{16,8},{24,16},{32,24},{40,32},{48,40},{56,48},{64,5... | collective-permute-start | bytes 1769480 | tf_op jit(solution)/shard_map/ppermute | solution.py:10
  161.9 3.1 copy-start.3
  161.9 3.1 copy-start.5
  166.1 542.7 %all-reduce.4.cloned.1.call-start = ((), (), s32[]{:S(2)}) async-start(), calls=%async_computation.3 | async-start | bytes 1048576 | tf_op jit(solution)/shard_map/psum | solution.py:49
  203.6 21.5 %collective-permute-start.4 = (bf16[6,192,256]{2,1,0:T(8,128)(2,1)}, bf16[6,192,256]{2,1,0:T(8,128)(2,1)}, u32[]{:S(2)}, u32[]{:S(2)}) collective-permute-start(bf16[6,192,256]{2,1,0:T(8,128)(2,1)} %gather_fusion.6), channel_id=1, source_target_pairs={{0,8},{8,16},{16,24},{24,32},{32,40},{40,48},{48,56},{56,64},{64,7... | collective-permute-start | bytes 1769480 | tf_op jit(solution)/shard_map/ppermute | solution.py:10
  209.8 19.3 %collective-permute-start.5 = (bf16[6,192,256]{2,1,0:T(8,128)(2,1)}, bf16[6,192,256]{2,1,0:T(8,128)(2,1)S(1)}, u32[]{:S(2)}, u32[]{:S(2)}) collective-permute-start(bf16[6,192,256]{2,1,0:T(8,128)(2,1)} %gather_fusion.7), channel_id=1, source_target_pairs={{0,504},{8,0},{16,8},{24,16},{32,24},{40,32},{48,40},{56,48},{64,5... | collective-permute-start | bytes 1769480 | tf_op jit(solution)/shard_map/ppermute | solution.py:10
  237.3 3.0 copy-start.1
  713.5 0.7 copy-start.6
Sparse Core Ops, SparseCore 0:
  10.7 38.9 all-gather.3
  90.7 34.3 all-gather.5
  166.2 34.2 all-gather.7
  242.4 466.3 all-reduce.3
where the time goes:
time: 816 us; the launch traced here: 814 us
  waiting for transfers between devices  606 us (74%)
  other arithmetic  85.1 us (10%)
  local copies, waits for them, and re-layouts  47.2 us (6%)
  starting transfers between devices  29.3 us (4%)
  matrix products  29 us (4%)
  between operations  18 us (2%)
    psum x1, waiting for transfers between devices, local(): gram, cross = lax.psum((gram_part, cross_part), ('region', 'split'))  466 us
    all_gather x3, waiting for transfers between devices, apply_blocks(): region = lax.all_gather(shard_blocks, 'split', axis=0, tiled=True)  108 us
    another operation x7, other arithmetic, local(): lower = jnp.linalg.cholesky(gram)  42.1 us
    ppermute x6, waiting for transfers between devices, shifted(): return lax.ppermute(value, axis, pairs)  30.8 us
    ppermute x6, starting transfers between devices, shifted(): return lax.ppermute(value, axis, pairs)  29.1 us
    another operation x3, other arithmetic, local(): jax.scipy.linalg.solve_triangular(lower, filtered_two.T, lower=True)  22.8 us
  transfers between devices with their start and end apart: 10, of which 10 were waited for; matrix products, arithmetic and copies ran while one was open for 2% of the time, Pallas kernels for 0%

commit v1 on v0

--- a/solution.py
+++ b/solution.py
@@ -2,6 +2,11 @@
 import jax.numpy as jnp
 from jax import lax
 from jax.sharding import PartitionSpec as P
+
+
+def one_after_other(x, inner_axis, outer_axis):
+    inner = lax.psum(x, inner_axis)
+    return lax.psum(inner, outer_axis)
 
 
 def shifted(value, axis, steps):
@@ -46,7 +51,7 @@
         filtered_two, filtered_two, contract, precision=lax.Precision.HIGHEST
     )
     cross_part = lax.dot_general(filtered_two, image, contract, precision=lax.Precision.HIGHEST)
-    gram, cross = lax.psum((gram_part, cross_part), ("region", "split"))
+    gram, cross = one_after_other((gram_part, cross_part), "split", "region")
     gram = gram / total_rows
     cross = cross / total_rows
     lower = jnp.linalg.cholesky(gram)

time: 816 us -> 697 us (0.85); the launches traced: 814 us -> 687 us
  waiting for transfers between devices: 606 us -> 478 us
    psum x1 -> x2, waiting for transfers between devices: 466 us -> 339 us  [the longest x1 263 us: one_after_other(): return lax.psum(inner, outer_axis)]
  transfers between devices with their start and end apart: 10 -> 11, of which waited for: 10 -> 11; matrix products, arithmetic and copies ran while one was open for 2% -> 2% of each run, Pallas kernels for 0% -> 0%
where the time goes in v1:
time: 697 us; the launch traced here: 687 us
  waiting for transfers between devices  478 us (69%)
  other arithmetic  84.8 us (12%)
  local copies, waits for them, and re-layouts  47.1 us (7%)
  starting transfers between devices  29.5 us (4%)
  matrix products  29 us (4%)
  between operations  17.8 us (3%)
    psum x1, waiting for transfers between devices, one_after_other(): return lax.psum(inner, outer_axis)  263 us
    all_gather x3, waiting for transfers between devices, apply_blocks(): region = lax.all_gather(shard_blocks, 'split', axis=0, tiled=True)  108 us
    psum x1, waiting for transfers between devices, one_after_other(): inner = lax.psum(x, inner_axis)  75.6 us
    another operation x7, other arithmetic, local(): lower = jnp.linalg.cholesky(gram)  42 us
    ppermute x6, waiting for transfers between devices, shifted(): return lax.ppermute(value, axis, pairs)  31.1 us
    ppermute x6, starting transfers between devices, shifted(): return lax.ppermute(value, axis, pairs)  29.1 us
    another operation x3, other arithmetic, local(): jax.scipy.linalg.solve_triangular(lower, filtered_two.T, lower=True)  22.8 us
    gather x3, local copies, waits for them, and re-layouts, apply_blocks(): picked = candidates[block_cols]  14.5 us
  transfers between devices with their start and end apart: 11, of which 11 were waited for; matrix products, arithmetic and copies ran while one was open for 2% of the time, Pallas kernels for 0%

profile of v1, /device:TPU:1, one launch (start us, length us, event | category | flops | bytes accessed | tf_op | source)
XLA Modules:
  0.0 686.5 jit_solution(2221420616518102281)
XLA Ops:
  7.2 2.0 convert_element_type.9
  10.1 39.6 %all-gather.4.cloned.1.call-done = bf16[24,192,256]{2,1,0:T(8,128)(2,1)} async-done(((bf16[3,192,256]{2,1,0:T(8,128)(2,1)}), bf16[24,192,256]{2,1,0:T(8,128)(2,1)}) %all-gather.4.cloned.1.call-update) | async-done | bytes 2359312 | tf_op jit(solution)/shard_map/all_gather | solution.py:23
  49.7 3.1 gather_fusion
  52.8 3.1 collective-permute-start
  55.9 3.1 gather_fusion.1
  59.0 6.6 collective-permute-start.1
  69.5 4.9 collective-permute-done
  74.3 4.0 collective-permute-done.1
  78.3 3.4 pad_maximum_fusion
  81.7 4.8 gather_fusion.2
  86.6 3.0 fusion.4
  89.6 0.9 fusion.19
  90.6 34.4 %all-gather.6.cloned.1.call-done = bf16[24,192,256]{2,1,0:T(8,128)(2,1)} async-done(((bf16[3,192,256]{2,1,0:T(8,128)(2,1)}), bf16[24,192,256]{2,1,0:T(8,128)(2,1)}) %all-gather.6.cloned.1.call-update) | async-done | bytes 2359312 | tf_op jit(solution)/shard_map/all_gather | solution.py:23
  125.0 3.1 gather_fusion.3
  128.1 3.1 collective-permute-start.2
  131.2 3.1 gather_fusion.4
  134.3 6.6 collective-permute-start.3
  140.9 8.7 %collective-permute-done.2 = bf16[6,192,256]{2,1,0:T(8,128)(2,1)} collective-permute-done((bf16[6,192,256]{2,1,0:T(8,128)(2,1)}, bf16[6,192,256]{2,1,0:T(8,128)(2,1)}, u32[]{:S(2)}, u32[]{:S(2)}) %collective-permute-start.2) | collective-permute-done | bytes 589856 | tf_op jit(solution)/shard_map/ppermute | solution.py:15
  149.6 4.0 collective-permute-done.3
  153.6 3.3 pad_maximum_fusion.1
  157.0 4.8 gather_fusion.5
  161.8 3.1 fusion.2
  164.9 1.1 fusion.38
  166.1 34.3 %all-gather.8.cloned.1.call-done = bf16[24,192,256]{2,1,0:T(8,128)(2,1)} async-done(((bf16[3,192,256]{2,1,0:T(8,128)(2,1)}), bf16[24,192,256]{2,1,0:T(8,128)(2,1)}) %all-gather.8.cloned.1.call-update) | async-done | bytes 2359312 | tf_op jit(solution)/shard_map/all_gather | solution.py:23
  200.4 3.1 gather_fusion.6
  203.5 3.1 collective-permute-start.4
  206.6 3.1 gather_fusion.7
  209.7 6.6 collective-permute-start.5
  216.3 3.2 fusion.42
  219.5 5.5 collective-permute-done.4
  225.0 4.0 collective-permute-done.5
  229.0 3.3 pad_maximum_fusion.2
  232.3 4.8 gather_fusion.8
  237.2 3.0 fusion
  240.2 2.0 fusion.43
  242.4 75.6 %all-reduce.8.cloned.1.call-done = (f32[256,256]{0,1:T(8,128)}, f32[256,256]{0,1:T(8,128)}) async-done(((f32[256,256]{0,1:T(8,128)}, f32[256,256]{0,1:T(8,128)}), (f32[256,256]{0,1:T(8,128)}, f32[256,256]{0,1:T(8,128)})) %all-reduce.8.cloned.1.call-update) | async-done | bytes 524304 | tf_op jit(solution)/shard_map/psum | solution.py:8
  318.1 263.2 %all-reduce.6.cloned.1.call-done = (f32[256,256]{0,1:T(8,128)}, f32[256,256]{0,1:T(8,128)}) async-done(((f32[256,256]{0,1:T(8,128)}, f32[256,256]{0,1:T(8,128)}), (f32[256,256]{0,1:T(8,128)}, f32[256,256]{0,1:T(8,128)})) %all-reduce.6.cloned.1.call-update) | async-done | bytes 524304 | tf_op jit(solution)/shard_map/psum | solution.py:9
  581.3 1.9 broadcast_multiply_fusion
  583.1 1.8 copy.13
  584.9 1.1 fusion.18
  587.3 13.2 %cholesky.50 = f32[128,128]{1,0:T(8,128)} custom-call(f32[128,128]{1,0:T(8,128)} %cholesky.118), custom_call_target="Cholesky" | custom-call | tf_op jit(solution)/shard_map/jit(cholesky)/cholesky | solution.py:57
  600.5 1.5 select_reduce_fusion.1
  602.0 1.6 cholesky.113
  603.5 11.3 %custom-call.18 = f32[1,128,128]{1,2,0:T(8,128)} custom-call(f32[1,128,128]{2,1,0:T(8,128)} %get-tuple-element.50), custom_call_target="InvertDiagBlocksLowerTriangular" | custom-call | tf_op jit(solution)/shard_map/jit(cholesky)/cholesky | solution.py:57
  614.8 1.7 constant_dynamic-update-slice_fusion.1
  616.5 1.7 convolution_subtract_fusion.3
  618.3 13.2 %cholesky.105 = f32[128,128]{1,0:T(8,128)} custom-call(f32[128,128]{1,0:T(8,128)} %convolution_subtract_fusion.3), custom_call_target="Cholesky" | custom-call | tf_op jit(solution)/shard_map/jit(cholesky)/cholesky | solution.py:57
  631.5 1.5 select_reduce_fusion
  635.6 1.7 select_select_fusion
  637.3 6.8 while.5
  637.9 2.8 bitcast_dynamic-update-slice_fusion.2
  641.4 2.8 bitcast_dynamic-update-slice_fusion.2
  644.2 21.1 %custom-call.19 = f32[2,128,128]{1,2,0:T(8,128)} custom-call(f32[2,128,128]{2,1,0:T(8,128)} %get-tuple-element.18), custom_call_target="InvertDiagBlocksLowerTriangular" | custom-call | tf_op jit(solution)/shard_map/jit(_solve_triangular)/triangular_solve | solution.py:58
  665.2 1.2 fusion.22
  666.5 1.3 convolution_subtract_fusion.2
  667.9 1.2 fusion.28
  669.0 1.2 fusion.20
  670.2 1.2 convolution_subtract_fusion.1
  671.4 1.2 fusion.27
  673.3 1.8 copy.15
  675.1 1.4 fusion.16
  676.5 1.4 convolution_subtract_fusion
  677.9 1.2 fusion.29
  679.2 0.9 maximum_bitcast_fusion
  (48 shorter events, 7.4 us)
Async XLA Ops:
  7.2 79.4 %copy-start = (bf16[3,12,192,192]{3,2,1,0:T(8,128)(2,1)S(1)}, bf16[3,12,192,192]{3,2,1,0:T(8,128)(2,1)}, u32[]{:S(2)}) copy-start(bf16[3,12,192,192]{3,2,1,0:T(8,128)(2,1)} %param.9) | copy-start | bytes 7962628
  7.2 58.4 %copy-start.8 = (f32[2]{0:T(128)S(1)}, f32[2]{0:T(128)}, u32[]{:S(2)}) copy-start(f32[2]{0:T(128)} %param.13) | copy-start | bytes 28
  7.2 61.4 %copy-start.7 = (s32[3,12]{1,0:T(4,128)S(1)}, s32[3,12]{1,0:T(4,128)}, u32[]{:S(2)}) copy-start(s32[3,12]{1,0:T(4,128)} %param.10) | copy-start | bytes 436
  7.2 42.5 %all-gather.4.cloned.1.call-start = ((), (), s32[]{:S(2)}) async-start(), calls=%async_computation | async-start | bytes 2654208 | tf_op jit(solution)/shard_map/all_gather | solution.py:23
  9.2 115.8 %all-gather.6.cloned.1.call-start = ((), (), s32[]{:S(2)}) async-start(), calls=%async_computation.1 | async-start | bytes 2654208 | tf_op jit(solution)/shard_map/all_gather | solution.py:23
  52.8 21.5 %collective-permute-start = (bf16[6,192,256]{2,1,0:T(8,128)(2,1)}, bf16[6,192,256]{2,1,0:T(8,128)(2,1)}, u32[]{:S(2)}, u32[]{:S(2)}) collective-permute-start(bf16[6,192,256]{2,1,0:T(8,128)(2,1)} %gather_fusion), channel_id=1, source_target_pairs={{0,8},{8,16},{16,24},{24,32},{32,40},{40,48},{48,56},{56,64},{64,7... | collective-permute-start | bytes 1769480 | tf_op jit(solution)/shard_map/ppermute | solution.py:15
  59.0 19.3 %collective-permute-start.1 = (bf16[6,192,256]{2,1,0:T(8,128)(2,1)}, bf16[6,192,256]{2,1,0:T(8,128)(2,1)}, u32[]{:S(2)}, u32[]{:S(2)}) collective-permute-start(bf16[6,192,256]{2,1,0:T(8,128)(2,1)} %gather_fusion.1), channel_id=1, source_target_pairs={{0,504},{8,0},{16,8},{24,16},{32,24},{40,32},{48,40},{56,48},{64,5... | collective-permute-start | bytes 1769480 | tf_op jit(solution)/shard_map/ppermute | solution.py:15
  86.6 3.1 copy-start.2
  89.6 0.9 copy-start.4
  90.5 109.9 %all-gather.8.cloned.1.call-start = ((), (), s32[]{:S(2)}) async-start(), calls=%async_computation.2 | async-start | bytes 2654208 | tf_op jit(solution)/shard_map/all_gather | solution.py:23
  128.1 21.5 %collective-permute-start.2 = (bf16[6,192,256]{2,1,0:T(8,128)(2,1)}, bf16[6,192,256]{2,1,0:T(8,128)(2,1)}, u32[]{:S(2)}, u32[]{:S(2)}) collective-permute-start(bf16[6,192,256]{2,1,0:T(8,128)(2,1)} %gather_fusion.3), channel_id=1, source_target_pairs={{0,8},{8,16},{16,24},{24,32},{32,40},{40,48},{48,56},{56,64},{64,7... | collective-permute-start | bytes 1769480 | tf_op jit(solution)/shard_map/ppermute | solution.py:15
  134.3 19.3 %collective-permute-start.3 = (bf16[6,192,256]{2,1,0:T(8,128)(2,1)}, bf16[6,192,256]{2,1,0:T(8,128)(2,1)S(1)}, u32[]{:S(2)}, u32[]{:S(2)}) collective-permute-start(bf16[6,192,256]{2,1,0:T(8,128)(2,1)} %gather_fusion.4), channel_id=1, source_target_pairs={{0,504},{8,0},{16,8},{24,16},{32,24},{40,32},{48,40},{56,48},{64,5... | collective-permute-start | bytes 1769480 | tf_op jit(solution)/shard_map/ppermute | solution.py:15
  161.8 3.1 copy-start.3
  161.8 3.1 copy-start.5
  166.0 152.0 %all-reduce.8.cloned.1.call-start = ((), (), s32[]{:S(2)}) async-start(), calls=%async_computation.4 | async-start | bytes 1048576 | tf_op jit(solution)/shard_map/psum | solution.py:8
  203.5 21.5 %collective-permute-start.4 = (bf16[6,192,256]{2,1,0:T(8,128)(2,1)}, bf16[6,192,256]{2,1,0:T(8,128)(2,1)}, u32[]{:S(2)}, u32[]{:S(2)}) collective-permute-start(bf16[6,192,256]{2,1,0:T(8,128)(2,1)} %gather_fusion.6), channel_id=1, source_target_pairs={{0,8},{8,16},{16,24},{24,32},{32,40},{40,48},{48,56},{56,64},{64,7... | collective-permute-start | bytes 1769480 | tf_op jit(solution)/shard_map/ppermute | solution.py:15
  209.7 19.3 %collective-permute-start.5 = (bf16[6,192,256]{2,1,0:T(8,128)(2,1)}, bf16[6,192,256]{2,1,0:T(8,128)(2,1)S(1)}, u32[]{:S(2)}, u32[]{:S(2)}) collective-permute-start(bf16[6,192,256]{2,1,0:T(8,128)(2,1)} %gather_fusion.7), channel_id=1, source_target_pairs={{0,504},{8,0},{16,8},{24,16},{32,24},{40,32},{48,40},{56,48},{64,5... | collective-permute-start | bytes 1769480 | tf_op jit(solution)/shard_map/ppermute | solution.py:15
  237.2 3.0 copy-start.1
  242.2 339.1 %all-reduce.6.cloned.1.call-start = ((), (), s32[]{:S(2)}) async-start(), calls=%async_computation.3 | async-start | bytes 1048576 | tf_op jit(solution)/shard_map/psum | solution.py:9
  586.0 0.7 copy-start.6
Sparse Core Ops, SparseCore 0:
  10.7 38.9 all-gather.3
  90.6 34.3 all-gather.5
  166.1 34.2 all-gather.7
  242.3 75.6 all-reduce.7
  321.3 259.8 all-reduce.5
